TPU v7x, 32 devices: a whole 2x2x4 slice. The times are simulated.
32 devices in a mesh: gx: 8 (over z, core), gy: 4 (over y, x).
Axes of the slice: x: 2, y: 2, z: 4, core: 2. Of those that a mesh axis runs over, the one named last changes fastest.
Arguments:
- offsets: float32 [384, 3, 128], P(('gx', 'gy')), may hold values from 0 to 1
- widths: float32 [384, 128], P(('gx', 'gy')), may hold values from 0.6 to 2.5
- solvation: float32 [384, 128], P(('gx', 'gy')), may hold values from -6 to 6
- heading: int32 [384, 1], P(('gx', 'gy')), may hold values from 0 to 8; in each aligned block of 12 rows (0 to 11, 12 to 23, ...) at most 3 rows name the same one
- old_map: float32 [64, 96, 1024], P('gx', 'gy'), may hold values from -6 to 6
Outputs:
- new_map: float32 [64, 96, 1024], P('gx', 'gy')
Inputs may be any that keep to these rules, and one draw needn't show every extreme that they name: `heading`: entry d moves a block d // 3 - 1 tiles along x and d % 3 - 1 tiles along y from the tile of the device that stores it; among the 12 blocks of one device at most 3 share an entry.
All inputs are finite; a program needn't handle non-finite values.
Results may differ from a plain program's by a relative error of at most 0.0003.
Values sent between devices are 32-bit elements; how exact they have to be, the bound alone decides.
A program may use at most 64 MiB of HBM per device.

v0:
```python
import jax
import jax.numpy as jnp
from jax import lax
from jax.sharding import PartitionSpec as P

SLOTS = 3
W = 5


def passed_along(value, axis, steps):
    count = lax.axis_size(axis)
    first, last = (max(0, -steps), min(count, count - steps))
    return lax.ppermute(value, axis, [(source, source + steps) for source in range(first, last)])


def block_field(rel, width_row, weight_row, span_x, span_y, span_z):
    alpha = 0.5 / (width_row * width_row)
    delta_x = span_x[None, :] - rel[0][:, None]
    delta_y = span_y[None, :] - rel[1][:, None]
    delta_z = span_z[None, :] - rel[2][:, None]
    along_x = jnp.exp(-alpha[:, None] * delta_x * delta_x)
    along_y = jnp.exp(-alpha[:, None] * delta_y * delta_y)
    along_z = jnp.exp(-alpha[:, None] * delta_z * delta_z)
    plane = weight_row[:, None, None] * along_x[:, :, None] * along_y[:, None, :]
    plane = plane.reshape(plane.shape[0], -1)
    return lax.dot_general(
        plane, along_z, (((0,), (0,)), ((), ())), precision=lax.Precision.HIGHEST
    )


def fold_rows(partial_value):
    core = partial_value[W : partial_value.shape[0] - W]
    for stride in (1, -1):
        edge = partial_value[partial_value.shape[0] - W :] if stride == 1 else partial_value[:W]
        landed = passed_along(edge, "gx", stride)
        if stride == 1:
            core = core.at[:W].add(landed)
        else:
            core = core.at[core.shape[0] - W :].add(landed)
    return core


def fold_cols(partial_value):
    core = partial_value[:, W : partial_value.shape[1] - W]
    for stride in (1, -1):
        edge = (
            partial_value[:, partial_value.shape[1] - W :] if stride == 1 else partial_value[:, :W]
        )
        landed = passed_along(edge, "gy", stride)
        if stride == 1:
            core = core.at[:, :W].add(landed)
        else:
            core = core.at[:, core.shape[1] - W :].add(landed)
    return core


def body(offsets, widths, solvation, heading, old_map):
    tile_x, tile_y, depth = old_map.shape
    stored = offsets.shape[0]
    lanes = offsets.shape[2]
    target = heading[:, 0]
    numbers = jnp.arange(stored)
    shared = target[:, None] == target[None, :]
    before = numbers[:, None] > numbers[None, :]
    order_rank = jnp.sum((shared & before).astype(jnp.int32), axis=1)
    slot_index = target * SLOTS + order_rank
    placing = (slot_index[:, None] == jnp.arange(9 * SLOTS)[None, :]).astype(jnp.float32)
    features = jnp.concatenate([offsets, widths[:, None, :], solvation[:, None, :]], axis=1)
    packed = jnp.einsum("bs,bkw->skw", placing, features, precision=lax.Precision.HIGHEST)
    packed = packed.reshape(3, 3, SLOTS, 5, lanes)
    filled = jnp.sum(placing, axis=0).reshape(3, 3, SLOTS)
    row_feats = [packed[0], packed[1], packed[2]]
    row_live = [filled[0], filled[1], filled[2]]
    for stride in (1, -1):
        moved = passed_along((packed[stride + 1], filled[stride + 1]), "gx", stride)
        row_feats[stride + 1] = moved[0]
        row_live[stride + 1] = moved[1]
    row_feats = jnp.stack(row_feats, axis=0)
    row_live = jnp.stack(row_live, axis=0)
    col_feats = [row_feats[:, 0], row_feats[:, 1], row_feats[:, 2]]
    col_live = [row_live[:, 0], row_live[:, 1], row_live[:, 2]]
    for stride in (1, -1):
        moved = passed_along((row_feats[:, stride + 1], row_live[:, stride + 1]), "gy", stride)
        col_feats[stride + 1] = moved[0]
        col_live[stride + 1] = moved[1]
    blocks = jnp.stack(col_feats, axis=0).reshape(9 * SLOTS, 5, lanes)
    present = jnp.stack(col_live, axis=0).reshape(9 * SLOTS)
    ext_x = tile_x + 2 * W
    ext_y = tile_y + 2 * W
    span_x = jnp.arange(ext_x).astype(jnp.float32) - W
    span_y = jnp.arange(ext_y).astype(jnp.float32) - W
    span_z = jnp.arange(depth).astype(jnp.float32)

    def accumulate(number, total):
        block = blocks[number]
        flag = present[number]
        rel = (block[0] * tile_x, block[1] * tile_y, block[2] * depth)
        width_row = block[3] + (1.0 - flag)
        return total + block_field(rel, width_row, block[4], span_x, span_y, span_z)

    empty = jnp.zeros((ext_x * ext_y, depth), jnp.float32)
    keys = ((1.0 - present) * 64.0).astype(jnp.int32) + jnp.arange(9 * SLOTS)
    arrange = jnp.argsort(keys, stable=True)
    blocks = blocks[arrange]
    present = present[arrange]
    count = jnp.sum(present).astype(jnp.int32)
    partial_value = lax.fori_loop(0, count, accumulate, empty)
    partial_value = partial_value.reshape(ext_x, ext_y, depth)
    core = fold_cols(fold_rows(partial_value))
    return old_map + core


def solution(mesh):
    placed = (
        P(("gx", "gy"), None, None),
        P(("gx", "gy"), None),
        P(("gx", "gy"), None),
        P(("gx", "gy"), None),
        P("gx", "gy", None),
    )
    return jax.shard_map(
        body, mesh=mesh, in_specs=placed, out_specs=P("gx", "gy", None), check_vma=False
    )
```

profile of v0, /device:TPU:10, one launch (start us, length us, event | category | flops | bytes accessed | tf_op | source)
XLA Modules:
  0.0 128.7 jit_solution(3848484548858438116)
XLA Ops:
  0.0 0.9 convert_reduce_fusion.1
  0.9 0.7 fusion.26
  1.8 1.9 %collective-permute-start.1 = (f32[3,3]{1,0:T(4,128)S(1)}, f32[3,3]{1,0:T(4,128)S(1)}, u32[]{:S(2)}, u32[]{:S(2)}) collective-permute-start(f32[3,3]{1,0:T(4,128)S(1)} %squeeze.33), channel_id=1, source_target_pairs={{0,4},{4,8},{8,12},{12,16},{16,20},{20,24},{24,28},{1,5},{5,9},{9,... | collective-permute-start | bytes 116 | tf_op jit(solution)/shard_map/ppermute | solution.py:13
  3.8 3.6 %collective-permute-start = (f32[3,3]{1,0:T(4,128)S(1)}, f32[3,3]{1,0:T(4,128)S(1)}, u32[]{:S(2)}, u32[]{:S(2)}) collective-permute-start(f32[3,3]{1,0:T(4,128)S(1)} %squeeze.32), channel_id=1, source_target_pairs={{4,0},{8,4},{12,8},{16,12},{20,16},{24,20},{28,24},{5,1},{9,5},{13... | collective-permute-start | bytes 116 | tf_op jit(solution)/shard_map/ppermute | solution.py:13
  7.5 0.7 copy.29
  8.2 1.0 fusion.16
  9.3 1.9 %collective-permute-start.5 = (f32[3,3,5,128]{3,2,1,0:T(8,128)S(1)}, f32[3,3,5,128]{3,2,1,0:T(8,128)S(1)}, u32[]{:S(2)}, u32[]{:S(2)}) collective-permute-start(f32[3,3,5,128]{3,2,1,0:T(8,128)S(1)} %bitcast.68), channel_id=1, source_target_pairs={{0,4},{4,8},{8,12},{12,16},{16,20},{20,24},{24,28},{1,5},{5,9},{9,... | collective-permute-start | bytes 69128 | tf_op jit(solution)/shard_map/ppermute | solution.py:13
  11.2 3.6 %collective-permute-start.4 = (f32[3,3,5,128]{3,2,1,0:T(8,128)S(1)}, f32[3,3,5,128]{3,2,1,0:T(8,128)S(1)}, u32[]{:S(2)}, u32[]{:S(2)}) collective-permute-start(f32[3,3,5,128]{3,2,1,0:T(8,128)S(1)} %bitcast.69), channel_id=1, source_target_pairs={{4,0},{8,4},{12,8},{16,12},{20,16},{24,20},{28,24},{5,1},{9,5},{13... | collective-permute-start | bytes 69128 | tf_op jit(solution)/shard_map/ppermute | solution.py:13
  15.0 3.4 %collective-permute-start.3 = (f32[3,3]{1,0:T(4,128)S(1)}, f32[3,3]{1,0:T(4,128)S(1)}, u32[]{:S(2)}, u32[]{:S(2)}) collective-permute-start(f32[3,3]{1,0:T(4,128)S(1)} %bitcast.73), channel_id=1, source_target_pairs={{0,1},{1,2},{2,3},{4,5},{5,6},{6,7},{8,9},{9,10},{10,11},{12,13},{... | collective-permute-start | bytes 116 | tf_op jit(solution)/shard_map/ppermute | solution.py:13
  18.4 2.4 %collective-permute-start.2 = (f32[3,3]{1,0:T(4,128)S(1)}, f32[3,3]{1,0:T(4,128)S(1)}, u32[]{:S(2)}, u32[]{:S(2)}) collective-permute-start(f32[3,3]{1,0:T(4,128)S(1)} %bitcast.72), channel_id=1, source_target_pairs={{1,0},{2,1},{3,2},{5,4},{6,5},{7,6},{9,8},{10,9},{11,10},{13,12},{... | collective-permute-start | bytes 116 | tf_op jit(solution)/shard_map/ppermute | solution.py:13
  20.9 3.9 %collective-permute-done.2 = f32[3,3]{1,0:T(4,128)S(1)} collective-permute-done((f32[3,3]{1,0:T(4,128)S(1)}, f32[3,3]{1,0:T(4,128)S(1)}, u32[]{:S(2)}, u32[]{:S(2)}) %collective-permute-start.2) | collective-permute-done | bytes 68 | tf_op jit(solution)/shard_map/ppermute | solution.py:13
  24.9 1.6 %sort.17 = (s32[27]{0:T(128)}, s32[27]{0:T(128)S(1)}) sort(s32[27]{0:T(128)S(1)} %iota_add_fusion, s32[27]{0:T(128)S(1)} %iota.28), dimensions={0}, to_apply=%region_2.0 | sort | flops 135 | bytes 432 | tf_op jit(solution)/shard_map/jit(argsort)/sort | solution.py:103
  26.6 1.9 %collective-permute-start.6 = (f32[3,3,5,128]{3,2,1,0:T(8,128)S(1)}, f32[3,3,5,128]{3,2,1,0:T(8,128)S(1)}, u32[]{:S(2)}, u32[]{:S(2)}) collective-permute-start(f32[3,3,5,128]{3,2,1,0:T(8,128)S(1)} %get-tuple-element.139), channel_id=1, source_target_pairs={{1,0},{2,1},{3,2},{5,4},{6,5},{7,6},{9,8},{10,9},{11,10},{13,12},{... | collective-permute-start | bytes 69128 | tf_op jit(solution)/shard_map/ppermute | solution.py:13
  28.5 4.8 %collective-permute-start.7 = (f32[3,3,5,128]{3,2,1,0:T(8,128)S(1)}, f32[3,3,5,128]{3,2,1,0:T(8,128)S(1)}, u32[]{:S(2)}, u32[]{:S(2)}) collective-permute-start(f32[3,3,5,128]{3,2,1,0:T(8,128)S(1)} %get-tuple-element.140), channel_id=1, source_target_pairs={{0,1},{1,2},{2,3},{4,5},{5,6},{6,7},{8,9},{9,10},{10,11},{12,13},{... | collective-permute-start | bytes 69128 | tf_op jit(solution)/shard_map/ppermute | solution.py:13
  33.4 0.7 gather_fusion
  34.1 0.6 reduce_sum.32
  36.2 50.6 %while.15 = (s32[]{:T(128)}, f32[612,1024]{1,0:T(8,128)S(1)}, s32[]{:T(128)}, f32[27,5,128]{2,1,0:T(8,128)S(1)}, f32[27]{0:T(128)S(1)}, /*index=5*/s32[]{:T(128)}, s32[]{:T(128)}, s32[]{:T(128)}, f32[1]{0:T(128)}) while((s32[]{:T(128)}, f32[612,1024]{1,0:T(8,128)S(1)}, s32[]{:T(128)}, f32[27,5,128]{2,1,0:T(8,128)S(1)}, ...), condition=%wide.region_5.6_spmd.clone, body=%wide.region_4.5_spmd.clone.sunk | while | flops 963715328 | bytes 6342727 | solution.py:107
  36.2 0.6 dynamic_slice.12
  37.7 2.7 %convolution_add_fusion.2 = f32[612,1024]{1,0:T(8,128)S(1)} fusion(f32[612,1024]{1,0:T(8,128)S(1)} %get-tuple-element.203, f32[128,612]{0,1:T(8,128)S(1)} %mul.223, f32[128]{0:T(128)S(1)} %get-tuple-element.192, f32[1024]{0:T(1024)S(1)} %iota_convert_fusion.2, f32[128]{0:T(128)S(1)} %get-tuple-element.189), kind=kOutput, calls=%fused_computation.5.clone.1 | convolution fusion | flops 963612672 | bytes 5331968 | tf_op jit(solution)/shard_map/while/body/dot_general | solution.py:26
  40.4 0.6 dynamic_slice.12
  41.9 2.7 %convolution_add_fusion.2 = f32[612,1024]{1,0:T(8,128)S(1)} fusion(f32[612,1024]{1,0:T(8,128)S(1)} %get-tuple-element.203, f32[128,612]{0,1:T(8,128)S(1)} %mul.223, f32[128]{0:T(128)S(1)} %get-tuple-element.192, f32[1024]{0:T(1024)S(1)} %iota_convert_fusion.2, f32[128]{0:T(128)S(1)} %get-tuple-element.189), kind=kOutput, calls=%fused_computation.5.clone.1 | convolution fusion | flops 963612672 | bytes 5331968 | tf_op jit(solution)/shard_map/while/body/dot_general | solution.py:26
  46.1 2.7 %convolution_add_fusion.2 = f32[612,1024]{1,0:T(8,128)S(1)} fusion(f32[612,1024]{1,0:T(8,128)S(1)} %get-tuple-element.203, f32[128,612]{0,1:T(8,128)S(1)} %mul.223, f32[128]{0:T(128)S(1)} %get-tuple-element.192, f32[1024]{0:T(1024)S(1)} %iota_convert_fusion.2, f32[128]{0:T(128)S(1)} %get-tuple-element.189), kind=kOutput, calls=%fused_computation.5.clone.1 | convolution fusion | flops 963612672 | bytes 5331968 | tf_op jit(solution)/shard_map/while/body/dot_general | solution.py:26
  50.3 2.7 %convolution_add_fusion.2 = f32[612,1024]{1,0:T(8,128)S(1)} fusion(f32[612,1024]{1,0:T(8,128)S(1)} %get-tuple-element.203, f32[128,612]{0,1:T(8,128)S(1)} %mul.223, f32[128]{0:T(128)S(1)} %get-tuple-element.192, f32[1024]{0:T(1024)S(1)} %iota_convert_fusion.2, f32[128]{0:T(128)S(1)} %get-tuple-element.189), kind=kOutput, calls=%fused_computation.5.clone.1 | convolution fusion | flops 963612672 | bytes 5331968 | tf_op jit(solution)/shard_map/while/body/dot_general | solution.py:26
  54.5 2.7 %convolution_add_fusion.2 = f32[612,1024]{1,0:T(8,128)S(1)} fusion(f32[612,1024]{1,0:T(8,128)S(1)} %get-tuple-element.203, f32[128,612]{0,1:T(8,128)S(1)} %mul.223, f32[128]{0:T(128)S(1)} %get-tuple-element.192, f32[1024]{0:T(1024)S(1)} %iota_convert_fusion.2, f32[128]{0:T(128)S(1)} %get-tuple-element.189), kind=kOutput, calls=%fused_computation.5.clone.1 | convolution fusion | flops 963612672 | bytes 5331968 | tf_op jit(solution)/shard_map/while/body/dot_general | solution.py:26
  58.7 2.7 %convolution_add_fusion.2 = f32[612,1024]{1,0:T(8,128)S(1)} fusion(f32[612,1024]{1,0:T(8,128)S(1)} %get-tuple-element.203, f32[128,612]{0,1:T(8,128)S(1)} %mul.223, f32[128]{0:T(128)S(1)} %get-tuple-element.192, f32[1024]{0:T(1024)S(1)} %iota_convert_fusion.2, f32[128]{0:T(128)S(1)} %get-tuple-element.189), kind=kOutput, calls=%fused_computation.5.clone.1 | convolution fusion | flops 963612672 | bytes 5331968 | tf_op jit(solution)/shard_map/while/body/dot_general | solution.py:26
  62.9 2.7 %convolution_add_fusion.2 = f32[612,1024]{1,0:T(8,128)S(1)} fusion(f32[612,1024]{1,0:T(8,128)S(1)} %get-tuple-element.203, f32[128,612]{0,1:T(8,128)S(1)} %mul.223, f32[128]{0:T(128)S(1)} %get-tuple-element.192, f32[1024]{0:T(1024)S(1)} %iota_convert_fusion.2, f32[128]{0:T(128)S(1)} %get-tuple-element.189), kind=kOutput, calls=%fused_computation.5.clone.1 | convolution fusion | flops 963612672 | bytes 5331968 | tf_op jit(solution)/shard_map/while/body/dot_general | solution.py:26
  67.2 2.7 %convolution_add_fusion.2 = f32[612,1024]{1,0:T(8,128)S(1)} fusion(f32[612,1024]{1,0:T(8,128)S(1)} %get-tuple-element.203, f32[128,612]{0,1:T(8,128)S(1)} %mul.223, f32[128]{0:T(128)S(1)} %get-tuple-element.192, f32[1024]{0:T(1024)S(1)} %iota_convert_fusion.2, f32[128]{0:T(128)S(1)} %get-tuple-element.189), kind=kOutput, calls=%fused_computation.5.clone.1 | convolution fusion | flops 963612672 | bytes 5331968 | tf_op jit(solution)/shard_map/while/body/dot_general | solution.py:26
  71.4 2.7 %convolution_add_fusion.2 = f32[612,1024]{1,0:T(8,128)S(1)} fusion(f32[612,1024]{1,0:T(8,128)S(1)} %get-tuple-element.203, f32[128,612]{0,1:T(8,128)S(1)} %mul.223, f32[128]{0:T(128)S(1)} %get-tuple-element.192, f32[1024]{0:T(1024)S(1)} %iota_convert_fusion.2, f32[128]{0:T(128)S(1)} %get-tuple-element.189), kind=kOutput, calls=%fused_computation.5.clone.1 | convolution fusion | flops 963612672 | bytes 5331968 | tf_op jit(solution)/shard_map/while/body/dot_general | solution.py:26
  75.6 2.7 %convolution_add_fusion.2 = f32[612,1024]{1,0:T(8,128)S(1)} fusion(f32[612,1024]{1,0:T(8,128)S(1)} %get-tuple-element.203, f32[128,612]{0,1:T(8,128)S(1)} %mul.223, f32[128]{0:T(128)S(1)} %get-tuple-element.192, f32[1024]{0:T(1024)S(1)} %iota_convert_fusion.2, f32[128]{0:T(128)S(1)} %get-tuple-element.189), kind=kOutput, calls=%fused_computation.5.clone.1 | convolution fusion | flops 963612672 | bytes 5331968 | tf_op jit(solution)/shard_map/while/body/dot_general | solution.py:26
  79.8 2.7 %convolution_add_fusion.2 = f32[612,1024]{1,0:T(8,128)S(1)} fusion(f32[612,1024]{1,0:T(8,128)S(1)} %get-tuple-element.203, f32[128,612]{0,1:T(8,128)S(1)} %mul.223, f32[128]{0:T(128)S(1)} %get-tuple-element.192, f32[1024]{0:T(1024)S(1)} %iota_convert_fusion.2, f32[128]{0:T(128)S(1)} %get-tuple-element.189), kind=kOutput, calls=%fused_computation.5.clone.1 | convolution fusion | flops 963612672 | bytes 5331968 | tf_op jit(solution)/shard_map/while/body/dot_general | solution.py:26
  84.0 2.7 %convolution_add_fusion.2 = f32[612,1024]{1,0:T(8,128)S(1)} fusion(f32[612,1024]{1,0:T(8,128)S(1)} %get-tuple-element.203, f32[128,612]{0,1:T(8,128)S(1)} %mul.223, f32[128]{0:T(128)S(1)} %get-tuple-element.192, f32[1024]{0:T(1024)S(1)} %iota_convert_fusion.2, f32[128]{0:T(128)S(1)} %get-tuple-element.189), kind=kOutput, calls=%fused_computation.5.clone.1 | convolution fusion | flops 963612672 | bytes 5331968 | tf_op jit(solution)/shard_map/while/body/dot_general | solution.py:26
  86.8 1.4 %fusion.28 = (f32[170,1024]{1,0:T(8,128)}, f32[170,1024]{1,0:T(8,128)}, f32[170,1024]{1,0:T(8,128)S(1)}) fusion(f32[612,1024]{1,0:T(8,128)S(1)} %get-tuple-element.98), kind=kLoop, calls=%fused_computation.63 | loop fusion | bytes 4177920 | tf_op jit(solution)/shard_map/slice | solution.py:34
  88.1 2.1 %slice.234 = f32[5,34,1024]{2,1,0:T(8,128)} reshape(f32[170,1024]{1,0:T(8,128)} %get-tuple-element.135) | data formatting | bytes 1392640 | tf_op jit(solution)/shard_map/slice | solution.py:34
  90.3 1.9 %collective-permute-start.8 = (f32[5,34,1024]{2,1,0:T(8,128)}, f32[5,34,1024]{2,1,0:T(8,128)}, u32[]{:S(2)}, u32[]{:S(2)}) collective-permute-start(f32[5,34,1024]{2,1,0:T(8,128)} %slice.234), channel_id=1, source_target_pairs={{0,4},{4,8},{8,12},{12,16},{16,20},{20,24},{24,28},{1,5},{5,9},{9,... | collective-permute-start | bytes 2088968 | tf_op jit(solution)/shard_map/ppermute | solution.py:13
  92.2 2.1 %slice.237 = f32[5,34,1024]{2,1,0:T(8,128)} reshape(f32[170,1024]{1,0:T(8,128)} %get-tuple-element.134) | data formatting | bytes 1392640 | tf_op jit(solution)/shard_map/slice | solution.py:34
  94.3 3.6 %collective-permute-start.9 = (f32[5,34,1024]{2,1,0:T(8,128)}, f32[5,34,1024]{2,1,0:T(8,128)}, u32[]{:S(2)}, u32[]{:S(2)}) collective-permute-start(f32[5,34,1024]{2,1,0:T(8,128)} %slice.237), channel_id=1, source_target_pairs={{4,0},{8,4},{12,8},{16,12},{20,16},{24,20},{28,24},{5,1},{9,5},{13... | collective-permute-start | bytes 2088968 | tf_op jit(solution)/shard_map/ppermute | solution.py:13
  97.9 1.1 slice.230
  99.0 1.4 %slice.231 = f32[8,34,1024]{2,1,0:T(8,128)S(1)} reshape(f32[272,1024]{1,0:T(8,128)} %slice.230) | data formatting | bytes 2228224 | tf_op jit(solution)/shard_map/slice | solution.py:32
  100.5 3.8 %collective-permute-done.8 = f32[5,34,1024]{2,1,0:T(8,128)} collective-permute-done((f32[5,34,1024]{2,1,0:T(8,128)}, f32[5,34,1024]{2,1,0:T(8,128)}, u32[]{:S(2)}, u32[]{:S(2)}) %collective-permute-start.8) | collective-permute-done | bytes 696352 | tf_op jit(solution)/shard_map/ppermute | solution.py:13
  104.2 1.2 add_dynamic-update-slice_fusion
  105.5 2.6 %collective-permute-done.9 = f32[5,34,1024]{2,1,0:T(8,128)} collective-permute-done((f32[5,34,1024]{2,1,0:T(8,128)}, f32[5,34,1024]{2,1,0:T(8,128)}, u32[]{:S(2)}, u32[]{:S(2)}) %collective-permute-start.9) | collective-permute-done | bytes 696352 | tf_op jit(solution)/shard_map/ppermute | solution.py:13
  108.1 1.4 %fusion.15 = f32[8,34,1024]{2,1,0:T(8,128)S(1)} fusion(f32[8,34,1024]{2,1,0:T(8,128)S(1)} %add_dynamic-update-slice_fusion, f32[5,34,1024]{2,1,0:T(8,128)} %collective-permute-done.9), kind=kLoop, calls=%fused_computation.28 | loop fusion | flops 174080 | bytes 2334720 | tf_op jit(solution)/shard_map/scatter-add | solution.py:39
  109.4 0.8 fusion.29
  110.2 4.8 %collective-permute-start.10 = (f32[8,5,1024]{2,1,0:T(8,128)S(1)}, f32[8,5,1024]{2,1,0:T(8,128)S(1)}, u32[]{:S(2)}, u32[]{:S(2)}) collective-permute-start(f32[8,5,1024]{2,1,0:T(8,128)S(1)} %get-tuple-element.138), channel_id=1, source_target_pairs={{0,1},{1,2},{2,3},{4,5},{5,6},{6,7},{8,9},{9,10},{10,11},{12,13},{... | collective-permute-start | bytes 491528 | tf_op jit(solution)/shard_map/ppermute | solution.py:13
  115.1 2.1 %collective-permute-start.11 = (f32[8,5,1024]{2,1,0:T(8,128)}, f32[8,5,1024]{2,1,0:T(8,128)S(1)}, u32[]{:S(2)}, u32[]{:S(2)}) collective-permute-start(f32[8,5,1024]{2,1,0:T(8,128)} %get-tuple-element.137), channel_id=1, source_target_pairs={{1,0},{2,1},{3,2},{5,4},{6,5},{7,6},{9,8},{10,9},{11,10},{13,12},{... | collective-permute-start | bytes 491528 | tf_op jit(solution)/shard_map/ppermute | solution.py:13
  117.2 3.6 %collective-permute-done.10 = f32[8,5,1024]{2,1,0:T(8,128)S(1)} collective-permute-done((f32[8,5,1024]{2,1,0:T(8,128)S(1)}, f32[8,5,1024]{2,1,0:T(8,128)S(1)}, u32[]{:S(2)}, u32[]{:S(2)}) %collective-permute-start.10) | collective-permute-done | bytes 163872 | tf_op jit(solution)/shard_map/ppermute | solution.py:13
  121.1 6.3 %collective-permute-done.11 = f32[8,5,1024]{2,1,0:T(8,128)S(1)} collective-permute-done((f32[8,5,1024]{2,1,0:T(8,128)}, f32[8,5,1024]{2,1,0:T(8,128)S(1)}, u32[]{:S(2)}, u32[]{:S(2)}) %collective-permute-start.11) | collective-permute-done | bytes 163872 | tf_op jit(solution)/shard_map/ppermute | solution.py:13
  127.8 1.0 add.72
  (157 shorter events, 11.1 us)
Async XLA Ops:
  1.8 13.1 %collective-permute-start.1 = (f32[3,3]{1,0:T(4,128)S(1)}, f32[3,3]{1,0:T(4,128)S(1)}, u32[]{:S(2)}, u32[]{:S(2)}) collective-permute-start(f32[3,3]{1,0:T(4,128)S(1)} %squeeze.33), channel_id=1, source_target_pairs={{0,4},{4,8},{8,12},{12,16},{16,20},{20,24},{24,28},{1,5},{5,9},{9,... | collective-permute-start | bytes 116 | tf_op jit(solution)/shard_map/ppermute | solution.py:13
  3.8 11.2 %collective-permute-start = (f32[3,3]{1,0:T(4,128)S(1)}, f32[3,3]{1,0:T(4,128)S(1)}, u32[]{:S(2)}, u32[]{:S(2)}) collective-permute-start(f32[3,3]{1,0:T(4,128)S(1)} %squeeze.32), channel_id=1, source_target_pairs={{4,0},{8,4},{12,8},{16,12},{20,16},{24,20},{28,24},{5,1},{9,5},{13... | collective-permute-start | bytes 116 | tf_op jit(solution)/shard_map/ppermute | solution.py:13
  9.3 17.3 %collective-permute-start.5 = (f32[3,3,5,128]{3,2,1,0:T(8,128)S(1)}, f32[3,3,5,128]{3,2,1,0:T(8,128)S(1)}, u32[]{:S(2)}, u32[]{:S(2)}) collective-permute-start(f32[3,3,5,128]{3,2,1,0:T(8,128)S(1)} %bitcast.68), channel_id=1, source_target_pairs={{0,4},{4,8},{8,12},{12,16},{16,20},{20,24},{24,28},{1,5},{5,9},{9,... | collective-permute-start | bytes 69128 | tf_op jit(solution)/shard_map/ppermute | solution.py:13
  11.2 15.3 %collective-permute-start.4 = (f32[3,3,5,128]{3,2,1,0:T(8,128)S(1)}, f32[3,3,5,128]{3,2,1,0:T(8,128)S(1)}, u32[]{:S(2)}, u32[]{:S(2)}) collective-permute-start(f32[3,3,5,128]{3,2,1,0:T(8,128)S(1)} %bitcast.69), channel_id=1, source_target_pairs={{4,0},{8,4},{12,8},{16,12},{20,16},{24,20},{28,24},{5,1},{9,5},{13... | collective-permute-start | bytes 69128 | tf_op jit(solution)/shard_map/ppermute | solution.py:13
  15.0 5.9 %collective-permute-start.3 = (f32[3,3]{1,0:T(4,128)S(1)}, f32[3,3]{1,0:T(4,128)S(1)}, u32[]{:S(2)}, u32[]{:S(2)}) collective-permute-start(f32[3,3]{1,0:T(4,128)S(1)} %bitcast.73), channel_id=1, source_target_pairs={{0,1},{1,2},{2,3},{4,5},{5,6},{6,7},{8,9},{9,10},{10,11},{12,13},{... | collective-permute-start | bytes 116 | tf_op jit(solution)/shard_map/ppermute | solution.py:13
  18.4 6.4 %collective-permute-start.2 = (f32[3,3]{1,0:T(4,128)S(1)}, f32[3,3]{1,0:T(4,128)S(1)}, u32[]{:S(2)}, u32[]{:S(2)}) collective-permute-start(f32[3,3]{1,0:T(4,128)S(1)} %bitcast.72), channel_id=1, source_target_pairs={{1,0},{2,1},{3,2},{5,4},{6,5},{7,6},{9,8},{10,9},{11,10},{13,12},{... | collective-permute-start | bytes 116 | tf_op jit(solution)/shard_map/ppermute | solution.py:13
  26.6 8.6 %collective-permute-start.6 = (f32[3,3,5,128]{3,2,1,0:T(8,128)S(1)}, f32[3,3,5,128]{3,2,1,0:T(8,128)S(1)}, u32[]{:S(2)}, u32[]{:S(2)}) collective-permute-start(f32[3,3,5,128]{3,2,1,0:T(8,128)S(1)} %get-tuple-element.139), channel_id=1, source_target_pairs={{1,0},{2,1},{3,2},{5,4},{6,5},{7,6},{9,8},{10,9},{11,10},{13,12},{... | collective-permute-start | bytes 69128 | tf_op jit(solution)/shard_map/ppermute | solution.py:13
  28.5 6.7 %collective-permute-start.7 = (f32[3,3,5,128]{3,2,1,0:T(8,128)S(1)}, f32[3,3,5,128]{3,2,1,0:T(8,128)S(1)}, u32[]{:S(2)}, u32[]{:S(2)}) collective-permute-start(f32[3,3,5,128]{3,2,1,0:T(8,128)S(1)} %get-tuple-element.140), channel_id=1, source_target_pairs={{0,1},{1,2},{2,3},{4,5},{5,6},{6,7},{8,9},{9,10},{10,11},{12,13},{... | collective-permute-start | bytes 69128 | tf_op jit(solution)/shard_map/ppermute | solution.py:13
  90.3 14.0 %collective-permute-start.8 = (f32[5,34,1024]{2,1,0:T(8,128)}, f32[5,34,1024]{2,1,0:T(8,128)}, u32[]{:S(2)}, u32[]{:S(2)}) collective-permute-start(f32[5,34,1024]{2,1,0:T(8,128)} %slice.234), channel_id=1, source_target_pairs={{0,4},{4,8},{8,12},{12,16},{16,20},{20,24},{24,28},{1,5},{5,9},{9,... | collective-permute-start | bytes 2088968 | tf_op jit(solution)/shard_map/ppermute | solution.py:13
  94.3 13.8 %collective-permute-start.9 = (f32[5,34,1024]{2,1,0:T(8,128)}, f32[5,34,1024]{2,1,0:T(8,128)}, u32[]{:S(2)}, u32[]{:S(2)}) collective-permute-start(f32[5,34,1024]{2,1,0:T(8,128)} %slice.237), channel_id=1, source_target_pairs={{4,0},{8,4},{12,8},{16,12},{20,16},{24,20},{28,24},{5,1},{9,5},{13... | collective-permute-start | bytes 2088968 | tf_op jit(solution)/shard_map/ppermute | solution.py:13
  110.2 10.6 %collective-permute-start.10 = (f32[8,5,1024]{2,1,0:T(8,128)S(1)}, f32[8,5,1024]{2,1,0:T(8,128)S(1)}, u32[]{:S(2)}, u32[]{:S(2)}) collective-permute-start(f32[8,5,1024]{2,1,0:T(8,128)S(1)} %get-tuple-element.138), channel_id=1, source_target_pairs={{0,1},{1,2},{2,3},{4,5},{5,6},{6,7},{8,9},{9,10},{10,11},{12,13},{... | collective-permute-start | bytes 491528 | tf_op jit(solution)/shard_map/ppermute | solution.py:13
  115.1 12.6 %copy-start = (f32[8,24,1024]{2,1,0:T(8,128)S(1)}, f32[8,24,1024]{2,1,0:T(8,128)}, u32[]{:S(2)}) copy-start(f32[8,24,1024]{2,1,0:T(8,128)} %param.19) | copy-start | bytes 2359300
  115.1 12.3 %collective-permute-start.11 = (f32[8,5,1024]{2,1,0:T(8,128)}, f32[8,5,1024]{2,1,0:T(8,128)S(1)}, u32[]{:S(2)}, u32[]{:S(2)}) collective-permute-start(f32[8,5,1024]{2,1,0:T(8,128)} %get-tuple-element.137), channel_id=1, source_target_pairs={{1,0},{2,1},{3,2},{5,4},{6,5},{7,6},{9,8},{10,9},{11,10},{13,12},{... | collective-permute-start | bytes 491528 | tf_op jit(solution)/shard_map/ppermute | solution.py:13
where the time goes:
time: 131 us; the launch traced here: 129 us
  starting transfers between devices  36.1 us (28%)
  matrix products  33.8 us (26%)
  waiting for transfers between devices  20.2 us (15%)
  local copies, waits for them, and re-layouts  19.7 us (15%)
  other arithmetic  10.2 us (8%)
  loops' own time  7.83 us (6%)
    ppermute x12, starting transfers between devices, passed_along(): lax.ppermute(value, axis, [(source, source + steps) for source in range(f...  36.1 us
    dot_general x12, matrix products, block_field(): lax.dot_general(plane, along_z, (((0,), (0,)), ((), ())), precision=lax.P...  32.8 us
    ppermute x12, waiting for transfers between devices, passed_along(): lax.ppermute(value, axis, [(source, source + steps) for source in range(f...  20.2 us
    another operation x1, loops' own time, body(): partial_value = lax.fori_loop(0, count, accumulate, empty)  7.83 us
    dynamic_slice x12, local copies, waits for them, and re-layouts, accumulate(): flag = present[number]  6.96 us
    slice x2, local copies, waits for them, and re-layouts, fold_rows(): partial_value[:W]  3.43 us
  transfers between devices with their start and end apart: 12, of which 5 were waited for; matrix products, arithmetic and copies ran while one was open for 9% of the time, Pallas kernels for 0%

commit v1 on v0

v1 whole, which is shorter than its diff:
```python
import functools
import math

import jax
import jax.numpy as jnp
from jax import lax
from jax.experimental import pallas as pl
from jax.experimental.pallas import tpu as pltpu
from jax.sharding import PartitionSpec as P

SLOTS = 3
W = 5
ROWS = 8
HOMES = (1, 0, 1, -1, 0, 1, -1, 0, -1)
ZTILE = 256
MESH = pl.DeviceIdType.MESH
VMEM = pl.BlockSpec(memory_space=pltpu.VMEM)
SMEM = pl.BlockSpec(memory_space=pltpu.SMEM)


def pack_kernel(heading, offsets, widths, solvation, packed, taken):
    packed[...] = jnp.zeros_like(packed)
    for number in range(9):
        taken[number] = 0
    lanes = offsets.shape[2]
    filled = jnp.ones((1, lanes), jnp.float32)
    rest = jnp.zeros((2, lanes), jnp.float32)
    for block in range(offsets.shape[0]):
        target = heading[block, 0]
        rank = taken[target]
        taken[target] = rank + 1
        slot = (lax.rem(target, 3) * 3 + lax.div(target, 3)) * SLOTS + rank
        packed[slot] = jnp.concatenate(
            [offsets[block], widths[pl.ds(block, 1)], solvation[pl.ds(block, 1)], filled, rest], axis=0
        )


def split(value):
    high = value.astype(jnp.bfloat16)
    return high, (value - high.astype(jnp.float32)).astype(jnp.bfloat16)


def field_kernel(rows, blocks, core, low_edge, high_edge, total, filled, slots, homes, sem):
    tile_x, tile_y, depth = core.shape
    lanes = blocks.shape[2]
    ext_y = tile_y + 2 * W
    fetch = pltpu.make_async_copy(blocks.at[:, 5], filled, sem)
    fetch.start()
    total[...] = jnp.zeros_like(total)
    fetch.wait()
    row = lax.axis_index("gx")
    per_home = filled.shape[0] // len(HOMES)
    count = jnp.int32(0)
    for group, home in enumerate(HOMES):
        within = ((row + home >= 0) & (row + home < rows)).astype(jnp.int32)
        for place in range(per_home):
            slot = group * per_home + place
            slots[count] = slot
            homes[count] = home
            count = count + within * filled[slot, 0].astype(jnp.int32)
    slots[count] = 0
    homes[count] = 0
    root = math.sqrt(0.5 * math.log2(math.e))
    row_x = lax.broadcasted_iota(jnp.int32, (tile_x, lanes), 0)

    def factors(number):
        live = jnp.where(number < count, 1.0, 0.0)
        block = blocks[slots[number]]
        home = homes[number]
        width = jnp.where(number < count, block[3:4], 1.0)
        scale = root / width
        pz = block[2:3] * depth
        columns = jnp.concatenate([scale, pz, block[2:8]], axis=0).T
        x0 = home * tile_x
        delta_x = (row_x - x0).astype(jnp.float32) - block[0:1] * tile_x
        tx = delta_x * scale
        exp_x = -(tx * tx)
        inside = (row_x >= x0 - W) & (row_x < x0 + tile_x + W)
        weight = jnp.where(inside, block[4:5] * live, 0.0)
        scale_full = jnp.broadcast_to(scale, (tile_x, lanes))
        start = -(W + block[1:2] * tile_y)
        start_full = jnp.broadcast_to(start, (tile_x, lanes))
        planes = []
        for j in range(ext_y):
            ty = (start_full + j) * scale_full
            planes.append(weight * jnp.exp2(exp_x - ty * ty))
        high, low = split(jnp.concatenate(planes, axis=0))
        return high, low, columns[:, 0:1], columns[:, 1:2]

    def accumulate(pair, carry):
        ah0, al0, s0, z0 = factors(2 * pair)
        ah1, al1, s1, z1 = factors(2 * pair + 1)
        plane = jnp.concatenate([ah0, ah1, al0, al1, ah0, ah1], axis=1)
        scale = jnp.concatenate([s0, s1], axis=0)
        centre = jnp.concatenate([z0, z1], axis=0)
        scale = jnp.broadcast_to(scale, (2 * lanes, ZTILE))
        centre = jnp.broadcast_to(centre, (2 * lanes, ZTILE))
        span = lax.broadcasted_iota(jnp.int32, (1, ZTILE), 1).astype(jnp.float32)
        for tile in range(depth // ZTILE):
            tz = ((span + tile * ZTILE) - centre) * scale
            zh, zl = split(jnp.exp2(-(tz * tz)))
            along_z = jnp.concatenate([zh, zh, zl], axis=0)
            out = jnp.dot(plane, along_z, preferred_element_type=jnp.float32)
            total[:, tile * ZTILE : (tile + 1) * ZTILE] += out
        return carry

    lax.fori_loop(0, lax.div(count + 1, 2), accumulate, 0)
    whole = total[...].reshape(ext_y, tile_x, depth)
    low_edge[...] = whole[:W]
    high_edge[...] = whole[ext_y - W :]
    core[...] = jnp.swapaxes(whole[W : ext_y - W], 0, 1)


def join_kernel(old_map, core, from_low, from_high, new_map):
    tile_y = core.shape[1]
    low = jnp.swapaxes(from_low[...], 0, 1)
    high = jnp.swapaxes(from_high[...], 0, 1)
    gap = jnp.zeros((core.shape[0], tile_y - 2 * W, core.shape[2]), jnp.float32)
    new_map[...] = old_map[...] + core[...] + jnp.concatenate([low, gap, high], axis=1)


def neighbours(rows, columns):
    row, column = lax.axis_index("gx"), lax.axis_index("gy")
    for step in (1, -1):
        yield 0, step, (column + step >= 0) & (column + step < columns)
    for step in (1, -1, 2, -2):
        yield step, 0, (row + step >= 0) & (row + step < rows)


def greet(links):
    row, column = lax.axis_index("gx"), lax.axis_index("gy")
    barrier = pltpu.get_barrier_semaphore()
    for dx, dy, there in links:

        @pl.when(there)
        def _():
            pl.semaphore_signal(barrier, 1, device_id=(row + dx, column + dy), device_id_type=MESH)

    pl.semaphore_wait(barrier, sum(there.astype(jnp.int32) for _, _, there in links))


def exchange_kernel(rows, columns, packed, blocks, own_sem, send_sem, recv_sem):
    row, column = lax.axis_index("gx"), lax.axis_index("gy")
    spans = {1: (1, 2, 6), -1: (0, 2, 1), 2: (2, 1, 8), -2: (0, 1, 0)}
    links = list(neighbours(rows, columns))
    for place, (dx, dy, there) in enumerate(links):

        @pl.when(jnp.logical_not(there))
        def _():
            if dx:
                first, number, group = spans[-dx]
                blocks[pl.ds(group, number)] = jnp.zeros((number,) + blocks.shape[1:], jnp.float32)
            else:
                blocks[pl.ds(3, 3), 1 - dy] = jnp.zeros((3,) + blocks.shape[2:], jnp.float32)

    greet(links)
    own = pltpu.make_async_copy(packed.at[1], blocks.at[pl.ds(3, 3), 1], own_sem)
    own.start()

    def copy(place):
        dx, dy, there = links[place]
        if dx:
            first, number, group = spans[dx]
            source, landing = blocks.at[pl.ds(3 + first, number)], blocks.at[pl.ds(group, number)]
        else:
            source, landing = packed.at[1 + dy], blocks.at[pl.ds(3, 3), 1 + dy]
        return pltpu.make_async_remote_copy(
            src_ref=source,
            dst_ref=landing,
            send_sem=send_sem.at[place],
            recv_sem=recv_sem.at[place],
            device_id=(row + dx, column + dy),
            device_id_type=MESH,
        )

    def arrived(place):
        dx, dy, _ = links[place]
        opposite = [there for x, y, there in links if (x, y) == (-dx, -dy)][0]

        @pl.when(opposite)
        def _():
            copy(place).wait_recv()

    def each(places, act):
        for place in places:

            @pl.when(links[place][2])
            def _():
                act(copy(place))

    each((0, 1), lambda c: c.start())
    own.wait()
    arrived(0)
    arrived(1)
    each((4, 5, 2, 3), lambda c: c.start())
    each((0, 1), lambda c: c.wait_send())
    for place in (2, 3, 4, 5):
        arrived(place)
    each((2, 3, 4, 5), lambda c: c.wait_send())


def edge_kernel(columns, low_edge, high_edge, from_low, from_high, send_sem, recv_sem):
    row, column = lax.axis_index("gx"), lax.axis_index("gy")
    links = [(0, 1, column + 1 < columns), (0, -1, column >= 1)]
    ends = [(high_edge, from_low), (low_edge, from_high)]
    for place, (_, _, there) in enumerate(links):

        @pl.when(jnp.logical_not(there))
        def _():
            landing = ends[1 - place][1]
            landing[...] = jnp.zeros_like(landing)

    greet(links)

    def copy(place):
        return pltpu.make_async_remote_copy(
            src_ref=ends[place][0],
            dst_ref=ends[place][1],
            send_sem=send_sem.at[place],
            recv_sem=recv_sem.at[place],
            device_id=(row, column + links[place][1]),
            device_id_type=MESH,
        )

    for place in (0, 1):

        @pl.when(links[place][2])
        def _():
            copy(place).start()

    for place in (0, 1):

        @pl.when(links[1 - place][2])
        def _():
            copy(place).wait_recv()

        @pl.when(links[place][2])
        def _():
            copy(place).wait_send()


def body(rows, columns, offsets, widths, solvation, heading, old_map):
    tile_x, tile_y, depth = old_map.shape
    lanes = offsets.shape[2]
    packed = pl.pallas_call(
        pack_kernel,
        out_shape=jax.ShapeDtypeStruct((9 * SLOTS, ROWS, lanes), jnp.float32),
        in_specs=[SMEM, VMEM, VMEM, VMEM],
        out_specs=VMEM,
        scratch_shapes=[pltpu.SMEM((9,), jnp.int32)],
    )(heading, offsets, widths, solvation)
    blocks = pl.pallas_call(
        functools.partial(exchange_kernel, rows, columns),
        out_shape=jax.ShapeDtypeStruct((len(HOMES), 3, SLOTS, ROWS, lanes), jnp.float32),
        in_specs=[VMEM],
        out_specs=VMEM,
        scratch_shapes=[
            pltpu.SemaphoreType.DMA,
            pltpu.SemaphoreType.DMA((6,)),
            pltpu.SemaphoreType.DMA((6,)),
        ],
        compiler_params=pltpu.CompilerParams(collective_id=0, has_side_effects=True),
    )(packed.reshape(3, 3, SLOTS, ROWS, lanes))
    blocks = blocks.reshape(-1, ROWS, lanes)
    number = blocks.shape[0]
    edge = jax.ShapeDtypeStruct((W, tile_x, depth), jnp.float32)
    core, low_edge, high_edge = pl.pallas_call(
        functools.partial(field_kernel, rows),
        out_shape=(jax.ShapeDtypeStruct(old_map.shape, jnp.float32), edge, edge),
        in_specs=[VMEM],
        out_specs=(VMEM, VMEM, VMEM),
        scratch_shapes=[
            pltpu.VMEM(((tile_y + 2 * W) * tile_x, depth), jnp.float32),
            pltpu.SMEM((number, lanes), jnp.float32),
            pltpu.SMEM((number + 2,), jnp.int32),
            pltpu.SMEM((number + 2,), jnp.int32),
            pltpu.SemaphoreType.DMA,
        ],
    )(blocks)
    from_low, from_high = pl.pallas_call(
        functools.partial(edge_kernel, columns),
        out_shape=(edge, edge),
        in_specs=[VMEM, VMEM],
        out_specs=(VMEM, VMEM),
        scratch_shapes=[pltpu.SemaphoreType.DMA((2,)), pltpu.SemaphoreType.DMA((2,))],
        compiler_params=pltpu.CompilerParams(collective_id=1, has_side_effects=True),
    )(low_edge, high_edge)
    return pl.pallas_call(
        join_kernel,
        out_shape=jax.ShapeDtypeStruct(old_map.shape, jnp.float32),
        in_specs=[VMEM] * 4,
        out_specs=VMEM,
    )(old_map, core, from_low, from_high)


def solution(mesh):
    placed = (
        P(("gx", "gy"), None, None),
        P(("gx", "gy"), None),
        P(("gx", "gy"), None),
        P(("gx", "gy"), None),
        P("gx", "gy", None),
    )
    return jax.shard_map(
        functools.partial(body, mesh.shape["gx"], mesh.shape["gy"]), mesh=mesh, in_specs=placed, out_specs=P("gx", "gy", None), check_vma=False
    )
```

time: 131 us -> 50.1 us (0.38); the launches traced: 129 us -> 49.8 us
  Pallas kernels: 0 us -> 48.5 us
  starting transfers between devices: 36.1 us -> 0 us
  matrix products: 33.8 us -> 0 us
  waiting for transfers between devices: 20.2 us -> 0 us
  local copies, waits for them, and re-layouts: 19.7 us -> 1.33 us
  other arithmetic: 10.2 us -> 0 us
  loops' own time: 7.83 us -> 0 us
    pallas_call x0 -> x5, Pallas kernels: none -> 48.5 us  [the longest x1 20.5 us: body(): pl.pallas_call(functools.partial(field_kernel, rows), out_shape=(jax.Shap...]
    ppermute x12 -> x0, starting transfers between devices: 36.1 us -> none  [passed_along(): lax.ppermute(value, axis, [(source, source + steps) for source in range(f...]
    dot_general x13 -> x0, matrix products: 33.8 us -> none  [the longest x12 32.8 us: block_field(): lax.dot_general(plane, along_z, (((0,), (0,)), ((), ())), precision=lax.P...]
    ppermute x12 -> x0, waiting for transfers between devices: 20.2 us -> none  [passed_along(): lax.ppermute(value, axis, [(source, source + steps) for source in range(f...]
    slice x13 -> x0, local copies, waits for them, and re-layouts: 9.12 us -> none  [the longest x2 3.43 us: fold_rows(): partial_value[:W]]
    another operation x1 -> x0, loops' own time: 7.83 us -> none  [body(): partial_value = lax.fori_loop(0, count, accumulate, empty)]
    dynamic_slice x24 -> x0, local copies, waits for them, and re-layouts: 7.08 us -> none  [the longest x12 6.96 us: accumulate(): flag = present[number]]
    scatter-add x2 -> x0, other arithmetic: 2.59 us -> none  [the longest x1 1.35 us: fold_rows(): core = core.at[core.shape[0] - W:].add(landed)]
  transfers between devices with their start and end apart: 12 -> 0, of which waited for: 5 -> 0; matrix products, arithmetic and copies ran while one was open for 9% -> 0% of each run, Pallas kernels for 0% -> 0%
where the time goes in v1:
time: 50.1 us; the launch traced here: 49.8 us
  Pallas kernels  48.5 us (97%)
  local copies, waits for them, and re-layouts  1.33 us (3%)
    pallas_call x1, Pallas kernels, body(): pl.pallas_call(functools.partial(field_kernel, rows), out_shape=(jax.Shap...  20.5 us
    pallas_call x1, Pallas kernels, body(): pl.pallas_call(functools.partial(edge_kernel, columns), out_shape=(edge,...  12.9 us
    pallas_call x1, Pallas kernels, body(): pl.pallas_call(functools.partial(exchange_kernel, rows, columns), out_sha...  10.9 us
    pallas_call x1, Pallas kernels, body(): pl.pallas_call(join_kernel, out_shape=jax.ShapeDtypeStruct(old_map.shape,...  2.5 us
    pallas_call x1, Pallas kernels, body(): pl.pallas_call(pack_kernel, out_shape=jax.ShapeDtypeStruct((9 * SLOTS, RO...  1.66 us
    unnamed x1, local copies, waits for them, and re-layouts  1.33 us

profile of v1, /device:TPU:10, one launch (start us, length us, event | category | flops | bytes accessed | tf_op | source)
XLA Modules:
  0.0 49.8 jit_solution(12349820700514221215)
XLA Ops:
  0.0 1.3 %copy.6.heading = s32[12,1]{1,0:T(8,128)} copy(s32[12,1]{0,1:T(1,128)} %param.8) | data formatting | bytes 96 | tf_op args[3]
  1.3 1.7 %shard_map.55 = f32[27,8,128]{2,1,0:T(8,128)} custom-call(s32[12,1]{1,0:T(8,128)} %copy.6.heading, f32[12,3,128]{2,1,0:T(4,128)} %offsets.1, f32[12,128]{1,0:T(8,128)} %widths.1, f32[12,128]{1,0:T(8,128)} %solvation.1), custom_call_target="tpu_custom_call" | custom-call | tf_op jit(solution)/shard_map/pallas_call | solution.py:245
  3.0 10.9 %shard_map.56 = f32[9,3,3,8,128]{4,3,2,1,0:T(8,128)} custom-call(f32[3,3,3,8,128]{4,3,2,1,0:T(8,128)} %bitcast.3), custom_call_target="tpu_custom_call" | custom-call | tf_op jit(solution)/shard_map/pallas_call | solution.py:252
  13.9 20.5 %shard_map.57 = (f32[8,24,1024]{2,1,0:T(8,128)}, f32[5,8,1024]{2,1,0:T(8,128)}, f32[5,8,1024]{2,1,0:T(8,128)}) custom-call(f32[81,8,128]{2,1,0:T(8,128)} %bitcast.2), custom_call_target="tpu_custom_call" | custom-call | tf_op jit(solution)/shard_map/pallas_call | solution.py:267
  34.4 12.9 %shard_map.58 = (f32[5,8,1024]{2,1,0:T(8,128)}, f32[5,8,1024]{2,1,0:T(8,128)}) custom-call(f32[5,8,1024]{2,1,0:T(8,128)} %get-tuple-element.11.low_edge, f32[5,8,1024]{2,1,0:T(8,128)} %get-tuple-element.12.high_edge), custom_call_target="tpu_custom_call" | custom-call | tf_op jit(solution)/shard_map/pallas_call | solution.py:280
  47.3 2.5 %shard_map.59 = f32[8,24,1024]{2,1,0:T(8,128)} custom-call(f32[8,24,1024]{2,1,0:T(8,128)} %old_map.1, f32[8,24,1024]{2,1,0:T(8,128)} %get-tuple-element.10.core, f32[5,8,1024]{2,1,0:T(8,128)} %get-tuple-element.13.from_low, f32[5,8,1024]{2,1,0:T(8,128)} %get-tuple-element.14.from_high), custom_call_target="tpu_custom_call" | custom-call | tf_op jit(solution)/shard_map/pallas_call | solution.py:288

commit v2 on v1

--- a/solution.py
+++ b/solution.py
@@ -10,7 +10,8 @@
 
 SLOTS = 3
 W = 5
-ROWS = 8
+FEATURES = 5
+ROWS = SLOTS * FEATURES + 1
 HOMES = (1, 0, 1, -1, 0, 1, -1, 0, -1)
 ZTILE = 256
 MESH = pl.DeviceIdType.MESH
@@ -23,16 +24,16 @@
     for number in range(9):
         taken[number] = 0
     lanes = offsets.shape[2]
-    filled = jnp.ones((1, lanes), jnp.float32)
-    rest = jnp.zeros((2, lanes), jnp.float32)
     for block in range(offsets.shape[0]):
-        target = heading[block, 0]
-        rank = taken[target]
-        taken[target] = rank + 1
-        slot = (lax.rem(target, 3) * 3 + lax.div(target, 3)) * SLOTS + rank
-        packed[slot] = jnp.concatenate(
-            [offsets[block], widths[pl.ds(block, 1)], solvation[pl.ds(block, 1)], filled, rest], axis=0
+        target = heading[block]
+        group = lax.rem(target, 3) * 3 + lax.div(target, 3)
+        rank = taken[group]
+        taken[group] = rank + 1
+        packed[group, pl.ds(rank * FEATURES, FEATURES)] = jnp.concatenate(
+            [offsets[block], widths[pl.ds(block, 1)], solvation[pl.ds(block, 1)]], axis=0
         )
+    for number in range(9):
+        packed[number, ROWS - 1 :] = jnp.full((1, lanes), taken[number].astype(jnp.float32))
 
 
 def split(value):
@@ -40,37 +41,41 @@
     return high, (value - high.astype(jnp.float32)).astype(jnp.bfloat16)
 
 
-def field_kernel(rows, blocks, core, low_edge, high_edge, total, filled, slots, homes, sem):
+def field_kernel(
+    rows, blocks, core, low_edge, high_edge, total, filled, groups, starts, homes, sem
+):
     tile_x, tile_y, depth = core.shape
     lanes = blocks.shape[2]
     ext_y = tile_y + 2 * W
-    fetch = pltpu.make_async_copy(blocks.at[:, 5], filled, sem)
+    fetch = pltpu.make_async_copy(blocks.at[:, ROWS - 1], filled, sem)
     fetch.start()
     total[...] = jnp.zeros_like(total)
     fetch.wait()
     row = lax.axis_index("gx")
-    per_home = filled.shape[0] // len(HOMES)
     count = jnp.int32(0)
-    for group, home in enumerate(HOMES):
-        within = ((row + home >= 0) & (row + home < rows)).astype(jnp.int32)
-        for place in range(per_home):
-            slot = group * per_home + place
-            slots[count] = slot
-            homes[count] = home
-            count = count + within * filled[slot, 0].astype(jnp.int32)
-    slots[count] = 0
+    for group in range(blocks.shape[0]):
+        home = HOMES[group // 3]
+        within = (row + home >= 0) & (row + home < rows)
+        number = jnp.where(within, filled[group, 0].astype(jnp.int32), 0)
+        for rank in range(SLOTS):
+            groups[count + rank] = group
+            starts[count + rank] = rank * FEATURES
+            homes[count + rank] = home
+        count = count + number
+    groups[count] = 0
+    starts[count] = 0
     homes[count] = 0
     root = math.sqrt(0.5 * math.log2(math.e))
     row_x = lax.broadcasted_iota(jnp.int32, (tile_x, lanes), 0)
 
     def factors(number):
         live = jnp.where(number < count, 1.0, 0.0)
-        block = blocks[slots[number]]
+        block = blocks[groups[number], pl.ds(starts[number], FEATURES)]
         home = homes[number]
         width = jnp.where(number < count, block[3:4], 1.0)
         scale = root / width
         pz = block[2:3] * depth
-        columns = jnp.concatenate([scale, pz, block[2:8]], axis=0).T
+        columns = jnp.concatenate([-scale * scale, pz, jnp.zeros((6, lanes), jnp.float32)], axis=0).T
         x0 = home * tile_x
         delta_x = (row_x - x0).astype(jnp.float32) - block[0:1] * tile_x
         tx = delta_x * scale
@@ -97,8 +102,8 @@
         centre = jnp.broadcast_to(centre, (2 * lanes, ZTILE))
         span = lax.broadcasted_iota(jnp.int32, (1, ZTILE), 1).astype(jnp.float32)
         for tile in range(depth // ZTILE):
-            tz = ((span + tile * ZTILE) - centre) * scale
-            zh, zl = split(jnp.exp2(-(tz * tz)))
+            delta_z = (span + tile * ZTILE) - centre
+            zh, zl = split(jnp.exp2(delta_z * delta_z * scale))
             along_z = jnp.concatenate([zh, zh, zl], axis=0)
             out = jnp.dot(plane, along_z, preferred_element_type=jnp.float32)
             total[:, tile * ZTILE : (tile + 1) * ZTILE] += out
@@ -244,14 +249,14 @@
     lanes = offsets.shape[2]
     packed = pl.pallas_call(
         pack_kernel,
-        out_shape=jax.ShapeDtypeStruct((9 * SLOTS, ROWS, lanes), jnp.float32),
+        out_shape=jax.ShapeDtypeStruct((9, ROWS, lanes), jnp.float32),
         in_specs=[SMEM, VMEM, VMEM, VMEM],
         out_specs=VMEM,
         scratch_shapes=[pltpu.SMEM((9,), jnp.int32)],
-    )(heading, offsets, widths, solvation)
+    )(heading[:, 0], offsets, widths, solvation)
     blocks = pl.pallas_call(
         functools.partial(exchange_kernel, rows, columns),
-        out_shape=jax.ShapeDtypeStruct((len(HOMES), 3, SLOTS, ROWS, lanes), jnp.float32),
+        out_shape=jax.ShapeDtypeStruct((len(HOMES), 3, ROWS, lanes), jnp.float32),
         in_specs=[VMEM],
         out_specs=VMEM,
         scratch_shapes=[
@@ -260,7 +265,7 @@
             pltpu.SemaphoreType.DMA((6,)),
         ],
         compiler_params=pltpu.CompilerParams(collective_id=0, has_side_effects=True),
-    )(packed.reshape(3, 3, SLOTS, ROWS, lanes))
+    )(packed.reshape(3, 3, ROWS, lanes))
     blocks = blocks.reshape(-1, ROWS, lanes)
     number = blocks.shape[0]
     edge = jax.ShapeDtypeStruct((W, tile_x, depth), jnp.float32)
@@ -272,8 +277,9 @@
         scratch_shapes=[
             pltpu.VMEM(((tile_y + 2 * W) * tile_x, depth), jnp.float32),
             pltpu.SMEM((number, lanes), jnp.float32),
-            pltpu.SMEM((number + 2,), jnp.int32),
-            pltpu.SMEM((number + 2,), jnp.int32),
+            pltpu.SMEM((number * SLOTS + SLOTS,), jnp.int32),
+            pltpu.SMEM((number * SLOTS + SLOTS,), jnp.int32),
+            pltpu.SMEM((number * SLOTS + SLOTS,), jnp.int32),
             pltpu.SemaphoreType.DMA,
         ],
     )(blocks)

time: 50.1 us -> 47.7 us (0.952)
  local copies, waits for them, and re-layouts: 1.33 us -> 0 us
  Pallas kernels: 48.5 us -> 47.3 us
    unnamed x1 -> x0, local copies, waits for them, and re-layouts: 1.33 us -> none
    pallas_call x1, Pallas kernels: 10.9 us -> 10.2 us  [body(): pl.pallas_call(functools.partial(exchange_kernel, rows, columns), out_sha...]
where the time goes in v2:
time: 47.7 us; the launch traced here: 47.4 us
  Pallas kernels  47.3 us (99%)
    pallas_call x1, Pallas kernels, body(): pl.pallas_call(functools.partial(field_kernel, rows), out_shape=(jax.Shap...  20.5 us
    pallas_call x1, Pallas kernels, body(): pl.pallas_call(functools.partial(edge_kernel, columns), out_shape=(edge,...  12.7 us
    pallas_call x1, Pallas kernels, body(): pl.pallas_call(functools.partial(exchange_kernel, rows, columns), out_sha...  10.2 us
    pallas_call x1, Pallas kernels, body(): pl.pallas_call(join_kernel, out_shape=jax.ShapeDtypeStruct(old_map.shape,...  2.5 us
    pallas_call x1, Pallas kernels, body(): pl.pallas_call(pack_kernel, out_shape=jax.ShapeDtypeStruct((9, ROWS, lane...  1.52 us

profile of v2, /device:TPU:10, one launch (start us, length us, event | category | flops | bytes accessed | tf_op | source)
XLA Modules:
  0.0 47.4 jit_solution(855572321101710430)
XLA Ops:
  0.0 1.5 %shard_map.55 = f32[9,16,128]{2,1,0:T(8,128)} custom-call(s32[12]{0:T(128)} %bitcast.5, f32[12,3,128]{2,1,0:T(4,128)} %offsets.1, f32[12,128]{1,0:T(8,128)} %widths.1, f32[12,128]{1,0:T(8,128)} %solvation.1), custom_call_target="tpu_custom_call" | custom-call | tf_op jit(solution)/shard_map/pallas_call | solution.py:250
  1.5 10.2 %shard_map.56 = f32[9,3,16,128]{3,2,1,0:T(8,128)} custom-call(f32[3,3,16,128]{3,2,1,0:T(8,128)} %bitcast.4), custom_call_target="tpu_custom_call" | custom-call | tf_op jit(solution)/shard_map/pallas_call | solution.py:257
  11.7 20.5 %shard_map.57 = (f32[8,24,1024]{2,1,0:T(8,128)}, f32[5,8,1024]{2,1,0:T(8,128)}, f32[5,8,1024]{2,1,0:T(8,128)}) custom-call(f32[27,16,128]{2,1,0:T(8,128)} %bitcast.3), custom_call_target="tpu_custom_call" | custom-call | tf_op jit(solution)/shard_map/pallas_call | solution.py:272
  32.2 12.7 %shard_map.58 = (f32[5,8,1024]{2,1,0:T(8,128)}, f32[5,8,1024]{2,1,0:T(8,128)}) custom-call(f32[5,8,1024]{2,1,0:T(8,128)} %get-tuple-element.11.low_edge, f32[5,8,1024]{2,1,0:T(8,128)} %get-tuple-element.12.high_edge), custom_call_target="tpu_custom_call" | custom-call | tf_op jit(solution)/shard_map/pallas_call | solution.py:286
  44.9 2.5 %shard_map.59 = f32[8,24,1024]{2,1,0:T(8,128)} custom-call(f32[8,24,1024]{2,1,0:T(8,128)} %old_map.1, f32[8,24,1024]{2,1,0:T(8,128)} %get-tuple-element.10.core, f32[5,8,1024]{2,1,0:T(8,128)} %get-tuple-element.13.from_low, f32[5,8,1024]{2,1,0:T(8,128)} %get-tuple-element.14.from_high), custom_call_target="tpu_custom_call" | custom-call | tf_op jit(solution)/shard_map/pallas_call | solution.py:294

commit v3 on v2

--- a/solution.py
+++ b/solution.py
@@ -116,14 +116,6 @@
     core[...] = jnp.swapaxes(whole[W : ext_y - W], 0, 1)
 
 
-def join_kernel(old_map, core, from_low, from_high, new_map):
-    tile_y = core.shape[1]
-    low = jnp.swapaxes(from_low[...], 0, 1)
-    high = jnp.swapaxes(from_high[...], 0, 1)
-    gap = jnp.zeros((core.shape[0], tile_y - 2 * W, core.shape[2]), jnp.float32)
-    new_map[...] = old_map[...] + core[...] + jnp.concatenate([low, gap, high], axis=1)
-
-
 def neighbours(rows, columns):
     row, column = lax.axis_index("gx"), lax.axis_index("gy")
     for step in (1, -1):
@@ -204,17 +196,13 @@
     each((2, 3, 4, 5), lambda c: c.wait_send())
 
 
-def edge_kernel(columns, low_edge, high_edge, from_low, from_high, send_sem, recv_sem):
+def edge_kernel(
+    columns, low_edge, high_edge, old_map, core, new_map, from_low, from_high, send_sem, recv_sem
+):
+    tile_y = core.shape[1]
     row, column = lax.axis_index("gx"), lax.axis_index("gy")
     links = [(0, 1, column + 1 < columns), (0, -1, column >= 1)]
     ends = [(high_edge, from_low), (low_edge, from_high)]
-    for place, (_, _, there) in enumerate(links):
-
-        @pl.when(jnp.logical_not(there))
-        def _():
-            landing = ends[1 - place][1]
-            landing[...] = jnp.zeros_like(landing)
-
     greet(links)
 
     def copy(place):
@@ -233,11 +221,14 @@
         def _():
             copy(place).start()
 
+    new_map[...] = old_map[...] + core[...]
     for place in (0, 1):
 
         @pl.when(links[1 - place][2])
         def _():
             copy(place).wait_recv()
+            first = 0 if place == 0 else tile_y - W
+            new_map[:, first : first + W] += jnp.swapaxes(ends[place][1][...], 0, 1)
 
         @pl.when(links[place][2])
         def _():
@@ -283,20 +274,19 @@
             pltpu.SemaphoreType.DMA,
         ],
     )(blocks)
-    from_low, from_high = pl.pallas_call(
+    return pl.pallas_call(
         functools.partial(edge_kernel, columns),
-        out_shape=(edge, edge),
-        in_specs=[VMEM, VMEM],
-        out_specs=(VMEM, VMEM),
-        scratch_shapes=[pltpu.SemaphoreType.DMA((2,)), pltpu.SemaphoreType.DMA((2,))],
-        compiler_params=pltpu.CompilerParams(collective_id=1, has_side_effects=True),
-    )(low_edge, high_edge)
-    return pl.pallas_call(
-        join_kernel,
         out_shape=jax.ShapeDtypeStruct(old_map.shape, jnp.float32),
         in_specs=[VMEM] * 4,
         out_specs=VMEM,
-    )(old_map, core, from_low, from_high)
+        scratch_shapes=[
+            pltpu.VMEM((W, tile_x, depth), jnp.float32),
+            pltpu.VMEM((W, tile_x, depth), jnp.float32),
+            pltpu.SemaphoreType.DMA((2,)),
+            pltpu.SemaphoreType.DMA((2,)),
+        ],
+        compiler_params=pltpu.CompilerParams(collective_id=1, has_side_effects=True),
+    )(low_edge, high_edge, old_map, core)
 
 
 def solution(mesh):

time: 47.7 us -> 48 us (level)
  local copies, waits for them, and re-layouts: 0 us -> 2.09 us
  Pallas kernels: 47.3 us -> 45.6 us
    unnamed x0 -> x1, local copies, waits for them, and re-layouts: none -> 2.09 us
    pallas_call x2 -> x1, Pallas kernels: 15.2 us -> 13.4 us  [body(): pl.pallas_call(functools.partial(edge_kernel, columns), out_shape=jax.Sha...]
where the time goes in v3:
time: 48 us; the launch traced here: 47.7 us
  Pallas kernels  45.6 us (95%)
  local copies, waits for them, and re-layouts  2.09 us (4%)
    pallas_call x1, Pallas kernels, body(): pl.pallas_call(functools.partial(field_kernel, rows), out_shape=(jax.Shap...  20.5 us
    pallas_call x1, Pallas kernels, body(): pl.pallas_call(functools.partial(edge_kernel, columns), out_shape=jax.Sha...  13.4 us
    pallas_call x1, Pallas kernels, body(): pl.pallas_call(functools.partial(exchange_kernel, rows, columns), out_sha...  10.2 us
    unnamed x1, local copies, waits for them, and re-layouts  2.09 us
    pallas_call x1, Pallas kernels, body(): pl.pallas_call(pack_kernel, out_shape=jax.ShapeDtypeStruct((9, ROWS, lane...  1.52 us

profile of v3, /device:TPU:10, one launch (start us, length us, event | category | flops | bytes accessed | tf_op | source)
XLA Modules:
  0.0 47.7 jit_solution(5157178652324930633)
XLA Ops:
  0.0 1.5 %shard_map.55 = f32[9,16,128]{2,1,0:T(8,128)} custom-call(s32[12]{0:T(128)} %bitcast.5, f32[12,3,128]{2,1,0:T(4,128)} %offsets.1, f32[12,128]{1,0:T(8,128)} %widths.1, f32[12,128]{1,0:T(8,128)} %solvation.1), custom_call_target="tpu_custom_call" | custom-call | tf_op jit(solution)/shard_map/pallas_call | solution.py:241
  1.5 10.2 %shard_map.56 = f32[9,3,16,128]{3,2,1,0:T(8,128)} custom-call(f32[3,3,16,128]{3,2,1,0:T(8,128)} %bitcast.4), custom_call_target="tpu_custom_call" | custom-call | tf_op jit(solution)/shard_map/pallas_call | solution.py:248
  11.7 20.5 %shard_map.57 = (f32[8,24,1024]{2,1,0:T(8,128)}, f32[5,8,1024]{2,1,0:T(8,128)}, f32[5,8,1024]{2,1,0:T(8,128)}) custom-call(f32[27,16,128]{2,1,0:T(8,128)} %bitcast.3), custom_call_target="tpu_custom_call" | custom-call | tf_op jit(solution)/shard_map/pallas_call | solution.py:263
  32.2 13.4 %shard_map.58 = f32[8,24,1024]{2,1,0:T(8,128)} custom-call(f32[5,8,1024]{2,1,0:T(8,128)} %get-tuple-element.8.low_edge, f32[5,8,1024]{2,1,0:T(8,128)} %get-tuple-element.9.high_edge, f32[8,24,1024]{2,1,0:T(8,128)} %old_map.1, f32[8,24,1024]{2,1,0:T(8,128)} %get-tuple-element.10.core), custom_call_target="tpu_custom_call" | custom-call | tf_op jit(solution)/shard_map/pallas_call | solution.py:277
  45.6 2.1 %copy.7 = f32[8,24,1024]{2,1,0:T(8,128)} copy(f32[8,24,1024]{2,1,0:T(8,128)} %shard_map.58) | data formatting | bytes 1572864
